TPU v7x, 512 devices: a whole 4x8x8 slice. The times are simulated.
512 devices in a mesh: feat: 128 (over x, y, z_hi), rows: 4 (over z_lo, core).
Axes of the slice: x: 4, y: 8, z: 8 (z_hi: 4, z_lo: 2; z = z_hi * 2 + z_lo), core: 2. Of those that a mesh axis runs over, the one named last changes fastest.
Arguments:
- binned: int32 [8192, 8192], P('rows', 'feat'), may hold values from 0 to 255
- node_of: int32 [8192], P('rows'), may hold values from 0 to 31
- margin: float32 [8192], P('rows'), may hold values from -6 to 6
- labels: float32 [8192], P('rows'), may hold values from 0 to 1
- split_feature: int32 [32], replicated, may hold values from 0 to 8191
- split_bin: int32 [32], replicated, may hold values from 0 to 255
Outputs:
- histogram: float32 [32, 2, 8192, 256], P('rows', None, 'feat')
- margin_out: float32 [8192], P('rows')
- child_out: int32 [8192], P('rows')
- grad_out: float32 [2, 8192], P(None, 'rows')
All inputs are finite; a program needn't handle non-finite values.
Results may differ from a plain program's by a relative error of at most 0.0045.
Values may be sent and summed in bfloat16 or wider, within the bound.
No kernel may reach another device: no remote copies, remote signals or barrier semaphores. Data moves between devices by JAX's collectives and lax.ppermute only.
A program may use at most 64 MiB of HBM per device.

v0:
```python
import jax
import jax.numpy as jnp
from jax import lax
from jax.sharding import PartitionSpec as P

BINS = 256


def leaf_table(selected, split_rows):
    below = (jnp.arange(selected.shape[2])[None, :] <= split_rows[:, None]).astype(jnp.float32)
    left = jnp.sum(selected * below[:, None, :], axis=2)
    whole = jnp.sum(selected, axis=2)
    return jnp.concatenate([left, whole], axis=1)


def node_sums(nodes_here, feature_ids, split_rows, feat_start):
    feat_count = nodes_here.shape[2]
    local = feature_ids - feat_start
    owned = (local >= 0) & (local < feat_count)
    chooser = ((local[:, None] == jnp.arange(feat_count)[None, :]) & owned[:, None]).astype(
        jnp.float32
    )
    selected = jnp.einsum("ncfb,nf->ncb", nodes_here, chooser, precision=lax.Precision.HIGHEST)
    return leaf_table(selected, split_rows)


def on_device(binned, node_of, margin, labels, split_feature, split_bin):
    row_count, feat_count = binned.shape
    node_total = split_feature.shape[0]
    feat_start = lax.axis_index("feat") * feat_count
    probability = jax.nn.sigmoid(margin)
    gradient = (probability - labels).astype(jnp.bfloat16)
    hessian = (probability * (1.0 - probability)).astype(jnp.bfloat16)
    node_hot = node_of[:, None] == jnp.arange(node_total, dtype=jnp.int32)[None, :]
    hot_float = node_hot.astype(jnp.bfloat16)
    weights = jnp.stack([gradient[:, None] * hot_float, hessian[:, None] * hot_float], axis=2)
    weights = weights.reshape(row_count, 2 * node_total)
    row_feature = jnp.sum(jnp.where(node_hot, split_feature[None, :], 0), axis=1)
    row_cut = jnp.sum(jnp.where(node_hot, split_bin[None, :], 0), axis=1)
    local = row_feature - feat_start
    owned = (local >= 0) & (local < feat_count)
    column_hot = jnp.arange(feat_count, dtype=jnp.int32)[None, :] == local[:, None]
    row_value = jnp.sum(jnp.where(column_hot, binned, 0), axis=1)
    right_bits = ((row_value > row_cut) & owned).astype(jnp.int32)
    go_right = lax.psum(right_bits, "feat")
    bin_ids = jnp.arange(BINS, dtype=jnp.int32)
    group = 8

    def add_block(block_index, partial_value):
        columns = lax.dynamic_slice_in_dim(binned, block_index * group, group, 1)
        one_hot = (columns.T[:, :, None] == bin_ids[None, None, :]).astype(jnp.bfloat16)
        piece = jnp.einsum("rk,frb->kfb", weights, one_hot, preferred_element_type=jnp.float32)
        return lax.dynamic_update_slice_in_dim(partial_value, piece, block_index * group, 1)

    partial_value = lax.fori_loop(
        0,
        feat_count // group,
        add_block,
        jnp.zeros((2 * node_total, feat_count, BINS), jnp.float32),
    )
    partial_value = partial_value.reshape(node_total, 2, feat_count, BINS).astype(jnp.bfloat16)
    node_share = node_total // lax.axis_size("rows")
    node_start = lax.axis_index("rows") * node_share
    summed = lax.psum(partial_value, "rows").astype(jnp.float32)
    histogram = lax.dynamic_slice_in_dim(summed, node_start, node_share, 0)
    table_part = node_sums(summed, split_feature, split_bin, feat_start)
    table = lax.psum(table_part, "feat")
    leaf_left = -table[:, 0] / (table[:, 1] + 1.0)
    leaf_right = -(table[:, 2] - table[:, 0]) / (table[:, 3] - table[:, 1] + 1.0)
    row_left = jnp.sum(jnp.where(node_hot, leaf_left[None, :], 0.0), axis=1)
    row_right = jnp.sum(jnp.where(node_hot, leaf_right[None, :], 0.0), axis=1)
    margin_out = margin + jnp.where(go_right == 1, row_right, row_left)
    child_out = 2 * node_of + go_right
    fresh = jax.nn.sigmoid(margin_out)
    grad_out = jnp.stack([fresh - labels, fresh * (1.0 - fresh)], axis=0)
    return (histogram, margin_out, child_out, grad_out)


def solution(mesh):
    in_specs = (P("rows", "feat"), P("rows"), P("rows"), P("rows"), P(), P())
    out_specs = (P("rows", None, "feat", None), P("rows"), P("rows"), P(None, "rows"))
    return jax.shard_map(
        on_device, mesh=mesh, in_specs=in_specs, out_specs=out_specs, check_vma=False
    )
```

profile of v0, /device:TPU:64, one launch (start us, length us, event | category | flops | bytes accessed | tf_op | source)
XLA Modules:
  0.0 510.7 jit_solution(691972997853340159)
XLA Ops:
  7.2 0.8 subtract_convert_fusion
  8.0 1.1 compare_select_fusion.1
  9.1 0.6 pad_maximum_fusion
  9.8 0.2 broadcast_in_dim.65
  10.1 35.7 %while.14 = (s32[]{:T(128)}, bf16[64,64,256]{2,0,1:T(8,128)(2,1)S(1)}, s32[2048,64]{0,1:T(8,128)S(1)}, bf16[2048,64]{0,1:T(8,128)(2,1)S(1)}, s32[]{:T(128)}, /*index=5*/s32[]{:T(128)}, s32[]{:T(128)}, s32[]{:T(128)}) while((s32[]{:T(128)}, bf16[64,64,256]{2,0,1:T(8,128)(2,1)S(1)}, s32[2048,64]{0,1:T(8,128)S(1)}, ...), condition=%wide.region_1.2_spmd.clone, body=%wide.region_0.1_spmd.clone.sunk | while | flops 541065216 | bytes 983187 | solution.py:55
  10.1 4.4 fusion.21
  14.6 4.4 fusion.21
  19.1 4.4 fusion.21
  23.5 4.4 fusion.21
  28.0 4.4 fusion.21
  32.5 4.4 fusion.21
  36.9 4.4 fusion.21
  41.4 4.4 fusion.21
  45.8 2.5 copy.11
  48.3 0.6 copy-done.1
  49.0 0.2 select_reduce_fusion.3
  49.3 34.9 %psum.22 = s32[2048]{0:T(1024)S(1)} all-reduce(s32[2048]{0:T(1024)S(1)} %and_convert_fusion), channel_id=1, replica_groups=mesh['feat'=128,'rows'=4] {'feat'}, use_global_device_ids=true, to_apply=%region_6.7 | all-reduce | flops 2048 | bytes 16384 | tf_op jit(solution)/shard_map/psum | solution.py:45
  84.2 0.6 multiply_add_fusion
  84.9 33.3 %all-reduce.2.cloned.1.call-done = bf16[32,2,64,256]{3,2,1,0:T(8,128)(2,1)} async-done(((bf16[32,2,64,256]{3,2,1,0:T(8,128)(2,1)}), bf16[32,2,64,256]{3,2,1,0:T(8,128)(2,1)}) %all-reduce.2.cloned.1.call-update) | async-done | bytes 2097168 | tf_op jit(solution)/shard_map/psum | solution.py:64
  118.2 2.0 fusion.8
  120.3 380.5 %psum.23 = f32[32,4]{0,1:T(4,128)S(1)} all-reduce(f32[32,4]{0,1:T(4,128)S(1)} %pad_maximum_fusion.2), channel_id=1, replica_groups=mesh['feat'=128,'rows'=4] {'feat'}, use_global_device_ids=true, to_apply=%region_9.10 | all-reduce | flops 128 | bytes 1024 | tf_op jit(solution)/shard_map/psum | solution.py:67
  500.8 0.2 select_reduce_fusion.1
  501.1 0.6 pad_maximum_fusion.1
  501.7 2.1 dynamic-slice_convert_fusion
  (35 shorter events, 0.7 us)
Async XLA Ops:
  7.2 2.9 copy-start
  7.2 111.0 %all-reduce.2.cloned.1.call-start = ((), (), s32[]{:S(2)}) async-start(), calls=%async_computation | async-start | bytes 4194304 | tf_op jit(solution)/shard_map/psum | solution.py:64
  48.3 0.7 copy-start.1
  48.3 0.7 copy-start.5
  48.3 0.7 copy-start.6
  48.3 452.7 %copy-start.2 = (f32[2048]{0:T(1024)S(1)}, f32[2048]{0:T(1024)}, u32[]{:S(2)}) copy-start(f32[2048]{0:T(1024)} %param.11) | copy-start | bytes 24580
  48.3 452.7 %copy-start.3 = (f32[2048]{0:T(1024)S(1)}, f32[2048]{0:T(1024)}, u32[]{:S(2)}) copy-start(f32[2048]{0:T(1024)} %param.10) | copy-start | bytes 24580
  501.0 2.8 copy-start.4
Sparse Core Ops, SparseCore 0:
  48.5 69.6 all-reduce.1
where the time goes:
time: 511 us
  blocking collectives  415 us (81%)
  matrix products  37.3 us (7%)
  waiting for transfers between devices  33.3 us (7%)
  between operations  14.2 us (3%)
  other arithmetic  6.54 us (1%)
    psum x1, blocking collectives, on_device(): table = lax.psum(table_part, 'feat')  381 us
    dot_general x8, matrix products, add_block(): jnp.einsum('rk,frb->kfb', weights, one_hot, preferred_element_type=jnp.fl...  35.3 us
    psum x1, blocking collectives, on_device(): go_right = lax.psum(right_bits, 'feat')  34.9 us
    psum x1, waiting for transfers between devices, on_device(): summed = lax.psum(partial_value, 'rows').astype(jnp.float32)  33.3 us
  transfers between devices with their start and end apart: 1, of which 1 were waited for; matrix products, arithmetic and copies ran while one was open for 0% of the time, Pallas kernels for 0%

commit v1 on v0

--- a/solution.py
+++ b/solution.py
@@ -4,6 +4,11 @@
 from jax.sharding import PartitionSpec as P
 
 BINS = 256
+
+
+def joints_process(mat):
+    z = lax.all_gather(mat, "feat").sum(axis=0)
+    return z
 
 
 def leaf_table(selected, split_rows):
@@ -64,7 +69,7 @@
     summed = lax.psum(partial_value, "rows").astype(jnp.float32)
     histogram = lax.dynamic_slice_in_dim(summed, node_start, node_share, 0)
     table_part = node_sums(summed, split_feature, split_bin, feat_start)
-    table = lax.psum(table_part, "feat")
+    table = joints_process(table_part)
     leaf_left = -table[:, 0] / (table[:, 1] + 1.0)
     leaf_right = -(table[:, 2] - table[:, 0]) / (table[:, 3] - table[:, 1] + 1.0)
     row_left = jnp.sum(jnp.where(node_hot, leaf_left[None, :], 0.0), axis=1)

time: 511 us -> 508 us (level)
    psum x1 -> x0, blocking collectives: 381 us -> none  [on_device(): table = lax.psum(table_part, 'feat')]
    all_gather x0 -> x1, blocking collectives: none -> 377 us  [joints_process(): z = lax.all_gather(mat, 'feat').sum(axis=0)]
where the time goes in v1:
time: 508 us
  blocking collectives  412 us (81%)
  matrix products  37.3 us (7%)
  waiting for transfers between devices  33.3 us (7%)
  between operations  14.2 us (3%)
  other arithmetic  6.68 us (1%)
    all_gather x1, blocking collectives, joints_process(): z = lax.all_gather(mat, 'feat').sum(axis=0)  377 us
    dot_general x8, matrix products, add_block(): jnp.einsum('rk,frb->kfb', weights, one_hot, preferred_element_type=jnp.fl...  35.3 us
    psum x1, blocking collectives, on_device(): go_right = lax.psum(right_bits, 'feat')  34.9 us
    psum x1, waiting for transfers between devices, on_device(): summed = lax.psum(partial_value, 'rows').astype(jnp.float32)  33.3 us
  transfers between devices with their start and end apart: 1, of which 1 were waited for; matrix products, arithmetic and copies ran while one was open for 0% of the time, Pallas kernels for 0%

profile of v1, /device:TPU:64, one launch (start us, length us, event | category | flops | bytes accessed | tf_op | source)
XLA Modules:
  0.0 507.7 jit_solution(5778854965331645247)
XLA Ops:
  7.2 0.8 subtract_convert_fusion
  8.0 1.1 compare_select_fusion.1
  9.1 0.6 pad_maximum_fusion
  9.8 0.2 broadcast_in_dim.65
  10.1 35.7 %while.14 = (s32[]{:T(128)}, bf16[64,64,256]{2,0,1:T(8,128)(2,1)S(1)}, s32[2048,64]{0,1:T(8,128)S(1)}, bf16[2048,64]{0,1:T(8,128)(2,1)S(1)}, s32[]{:T(128)}, /*index=5*/s32[]{:T(128)}, s32[]{:T(128)}, s32[]{:T(128)}) while((s32[]{:T(128)}, bf16[64,64,256]{2,0,1:T(8,128)(2,1)S(1)}, s32[2048,64]{0,1:T(8,128)S(1)}, ...), condition=%wide.region_1.2_spmd.clone, body=%wide.region_0.1_spmd.clone.sunk | while | flops 541065216 | bytes 983187 | solution.py:60
  10.1 4.4 fusion.21
  14.6 4.4 fusion.21
  19.1 4.4 fusion.21
  23.5 4.4 fusion.21
  28.0 4.4 fusion.21
  32.5 4.4 fusion.21
  36.9 4.4 fusion.21
  41.4 4.4 fusion.21
  45.8 2.5 copy.12
  48.4 0.6 copy-done.1
  49.0 0.2 select_reduce_fusion.3
  49.3 34.9 %psum.15 = s32[2048]{0:T(1024)S(1)} all-reduce(s32[2048]{0:T(1024)S(1)} %and_convert_fusion), channel_id=1, replica_groups=mesh['feat'=128,'rows'=4] {'feat'}, use_global_device_ids=true, to_apply=%region_6.7 | all-reduce | flops 2048 | bytes 16384 | tf_op jit(solution)/shard_map/psum | solution.py:50
  84.2 0.6 multiply_add_fusion
  84.9 33.3 %all-reduce.2.cloned.1.call-done = bf16[32,2,64,256]{3,2,1,0:T(8,128)(2,1)} async-done(((bf16[32,2,64,256]{3,2,1,0:T(8,128)(2,1)}), bf16[32,2,64,256]{3,2,1,0:T(8,128)(2,1)}) %all-reduce.2.cloned.1.call-update) | async-done | bytes 2097168 | tf_op jit(solution)/shard_map/psum | solution.py:69
  118.2 2.0 fusion.8
  120.3 377.4 %all-gather.1 = f32[128,32,4]{1,2,0:T(4,128)S(1)} all-gather(f32[1,32,4]{1,2,0:T(4,128)S(1)} %maximum_bitcast_fusion), channel_id=2, replica_groups=mesh['feat'=128,'rows'=4] {'feat'}, dimensions={0}, use_global_device_ids=true | all-gather | bytes 66048 | tf_op jit(solution)/shard_map/all_gather | solution.py:10
  497.9 0.2 select_reduce_fusion.1
  498.1 0.6 pad_maximum_fusion.1
  498.7 2.1 dynamic-slice_convert_fusion
  (36 shorter events, 0.8 us)
Async XLA Ops:
  7.2 2.9 copy-start
  7.2 111.0 %all-reduce.2.cloned.1.call-start = ((), (), s32[]{:S(2)}) async-start(), calls=%async_computation | async-start | bytes 4194304 | tf_op jit(solution)/shard_map/psum | solution.py:69
  48.3 0.7 copy-start.1
  48.3 0.7 copy-start.5
  48.3 0.7 copy-start.6
  48.3 449.7 %copy-start.2 = (f32[2048]{0:T(1024)S(1)}, f32[2048]{0:T(1024)}, u32[]{:S(2)}) copy-start(f32[2048]{0:T(1024)} %param.11) | copy-start | bytes 24580
  48.3 449.7 %copy-start.3 = (f32[2048]{0:T(1024)S(1)}, f32[2048]{0:T(1024)}, u32[]{:S(2)}) copy-start(f32[2048]{0:T(1024)} %param.10) | copy-start | bytes 24580
  498.1 2.8 copy-start.4
Sparse Core Ops, SparseCore 0:
  48.4 69.6 all-reduce.1
